TPU v7x, 256 devices: a whole 4x4x8 slice. The times are simulated.
256 devices in a mesh: gx: 8 (over y, core), gy: 32 (over x, z).
Axes of the slice: x: 4, y: 4, z: 8, core: 2. Of those that a mesh axis runs over, the one named last changes fastest.
Arguments:
- flow_field: float32 [16, 256, 256, 128], P(None, 'gx', 'gy'), may hold values from -6 to 6
- cotangent: float32 [16, 256, 256, 128], P(None, 'gx', 'gy'), may hold values from -6 to 6
- mode_weights: float32 [4, 16, 16, 256], replicated, may hold values from -3 to 3
- point_weights: float32 [16, 16], replicated, may hold values from -1.5 to 1.5
- point_bias: float32 [16], replicated, may hold values from -3 to 3
Outputs:
- output_field: float32 [16, 256, 256, 128], P(None, 'gx', 'gy')
- grad_field: float32 [16, 256, 256, 128], P(None, 'gx', 'gy')
- grad_modes: float32 [4, 16, 16, 256], replicated
- grad_point: float32 [16, 16], replicated
- grad_bias: float32 [16], replicated
All inputs are finite; a program needn't handle non-finite values.
Results may differ from a plain program's by a relative error of at most 0.00024.
Values sent between devices are 32-bit elements; how exact they have to be, the bound alone decides.
No kernel may reach another device: no remote copies, remote signals or barrier semaphores. Data moves between devices by JAX's collectives and lax.ppermute only.
A program may use at most 128 MiB of HBM per device.

v0:
```python
import math
import jax
import jax.numpy as jnp
from jax import lax
from jax.sharding import PartitionSpec as P

LOW_PASS = [
    0.23037781330885523,
    0.7148465705525415,
    0.6308807679295904,
    -0.02798376941698385,
    -0.18703481171888114,
    0.030841381835986965,
    0.032883011666982945,
    -0.010597401784997278,
]
HIGH_PASS = [(-1) ** position * LOW_PASS[7 - position] for position in range(8)]
GELU_SCALE = 0.7978845608028654
GELU_CUBE = 0.044715


def from_behind(value, axis, by):
    devices = lax.axis_size(axis)
    return lax.ppermute(value, axis, [(i, (i + by) % devices) for i in range(devices)])


def filter_table(filter_taps, out_count, in_count, periodic):
    row_index = lax.broadcasted_iota(jnp.int32, (out_count, in_count), 0)
    col_index = lax.broadcasted_iota(jnp.int32, (out_count, in_count), 1)
    offset = col_index - 2 * row_index
    if periodic:
        offset = offset % in_count
    matrix = jnp.zeros((out_count, in_count), jnp.float32)
    for position in range(8):
        matrix = matrix + filter_taps[position] * (offset == position).astype(jnp.float32)
    return matrix


def lifted_table(filter_taps, out_count, in_count):
    row_index = lax.broadcasted_iota(jnp.int32, (out_count, in_count), 0)
    col_index = lax.broadcasted_iota(jnp.int32, (out_count, in_count), 1)
    offset = row_index - 2 * col_index + 6
    matrix = jnp.zeros((out_count, in_count), jnp.float32)
    for position in range(8):
        matrix = matrix + filter_taps[position] * (offset == position).astype(jnp.float32)
    return matrix


def along_x(matrix, signal):
    return jnp.einsum("kr,arys->akys", matrix, signal, precision=lax.Precision.HIGHEST)


def along_y(matrix, signal):
    return jnp.einsum("kr,axrs->axks", matrix, signal, precision=lax.Precision.HIGHEST)


def plane_x(matrix, signal):
    return jnp.einsum("kr,ary->aky", matrix, signal, precision=lax.Precision.HIGHEST)


def plane_y(matrix, signal):
    return jnp.einsum("kr,axr->axk", matrix, signal, precision=lax.Precision.HIGHEST)


def to_lanes(signal):
    channels, extent_x, extent_y, planes = signal.shape
    return jnp.transpose(signal, (0, 3, 1, 2)).reshape(channels * planes, extent_x, extent_y)


def from_lanes(signal, channels):
    stacked, extent_x, extent_y = signal.shape
    return jnp.transpose(
        signal.reshape(channels, stacked // channels, extent_x, extent_y), (0, 2, 3, 1)
    )


def four_bands(signal):
    extent_x, extent_y = (signal.shape[1], signal.shape[2])
    low_x = plane_x(filter_table(LOW_PASS, extent_x // 2, extent_x, True), signal)
    high_x = plane_x(filter_table(HIGH_PASS, extent_x // 2, extent_x, True), signal)
    low_y = filter_table(LOW_PASS, extent_y // 2, extent_y, True)
    high_y = filter_table(HIGH_PASS, extent_y // 2, extent_y, True)
    return jnp.stack(
        [
            plane_y(low_y, low_x),
            plane_y(low_y, high_x),
            plane_y(high_y, low_x),
            plane_y(high_y, high_x),
        ]
    )


def join_bands(changes):
    modes_x, modes_y = (changes.shape[2], changes.shape[3])
    low_x = filter_table(LOW_PASS, modes_x, 2 * modes_x, True).T
    high_x = filter_table(HIGH_PASS, modes_x, 2 * modes_x, True).T
    low_y = filter_table(LOW_PASS, modes_y, 2 * modes_y, True).T
    high_y = filter_table(HIGH_PASS, modes_y, 2 * modes_y, True).T
    from_low = plane_y(low_y, changes[0]) + plane_y(high_y, changes[2])
    from_high = plane_y(low_y, changes[1]) + plane_y(high_y, changes[3])
    return plane_x(low_x, from_low) + plane_x(high_x, from_high)


def gelu_parts(signal):
    tangent = jnp.tanh(GELU_SCALE * (signal + GELU_CUBE * signal * signal * signal))
    activated = 0.5 * signal * (1.0 + tangent)
    gelu_slope = 0.5 * (1.0 + tangent) + 0.5 * signal * (1.0 - tangent * tangent) * GELU_SCALE * (
        1.0 + 3.0 * GELU_CUBE * signal * signal
    )
    return (activated, gelu_slope)


def wave_block(signal, weights_grid, transposed):
    x_index = lax.axis_index("gx")
    channels = signal.shape[0]
    extent_x, extent_y = (signal.shape[1], signal.shape[2])
    margin = from_behind(signal[:, :6], "gx", -1)
    halved = along_x(
        filter_table(LOW_PASS, extent_x // 2, extent_x + 6, False),
        jnp.concatenate([signal, margin], 1),
    )
    margin = from_behind(halved[:, :, :6], "gy", -1)
    level_one = along_y(
        filter_table(LOW_PASS, extent_y // 2, extent_y + 6, False),
        jnp.concatenate([halved, margin], 2),
    )
    level_one = to_lanes(lax.all_to_all(level_one, "gy", split_axis=3, concat_axis=2, tiled=True))
    rows_one, cols_one = (level_one.shape[1], level_one.shape[2])
    margin = from_behind(level_one[:, :6], "gx", -1)
    level_two = plane_x(
        filter_table(LOW_PASS, rows_one // 2, rows_one + 6, False),
        jnp.concatenate([level_one, margin], 1),
    )
    level_two = plane_y(filter_table(LOW_PASS, cols_one // 2, cols_one, True), level_two)
    rows_two, cols_two = (level_two.shape[1], level_two.shape[2])
    margin = from_behind(level_two[:, :6], "gx", -1)
    level_three = plane_x(
        filter_table(LOW_PASS, rows_two // 2, rows_two + 6, False),
        jnp.concatenate([level_two, margin], 1),
    )
    level_three = plane_y(filter_table(LOW_PASS, cols_two // 2, cols_two, True), level_three)
    gathered = lax.all_gather(level_three, "gx", axis=1, tiled=True)
    wave_bands = four_bands(gathered)
    stacked, modes_x, modes_y = (wave_bands.shape[1], wave_bands.shape[2], wave_bands.shape[3])
    split_bands = wave_bands.reshape(4, channels, stacked // channels, modes_x, modes_y)
    if transposed:
        mixed_bands = jnp.einsum(
            "bozxy,bioxy->bizxy", split_bands, weights_grid, precision=lax.Precision.HIGHEST
        )
    else:
        mixed_bands = jnp.einsum(
            "bizxy,bioxy->bozxy", split_bands, weights_grid, precision=lax.Precision.HIGHEST
        )
    delta_three = join_bands((mixed_bands - split_bands).reshape(4, stacked, modes_x, modes_y))
    own_rows = rows_two // 2
    own_part = lax.dynamic_slice_in_dim(delta_three, x_index * own_rows, own_rows, 1)
    margin = from_behind(own_part[:, own_rows - 3 :], "gx", 1)
    delta_two = plane_x(
        lifted_table(LOW_PASS, 2 * own_rows, own_rows + 3), jnp.concatenate([margin, own_part], 1)
    )
    cols_three = own_part.shape[2]
    delta_two = plane_y(filter_table(LOW_PASS, cols_three, 2 * cols_three, True).T, delta_two)
    margin = from_behind(delta_two[:, rows_two - 3 :], "gx", 1)
    delta_one = plane_x(
        lifted_table(LOW_PASS, 2 * rows_two, rows_two + 3), jnp.concatenate([margin, delta_two], 1)
    )
    delta_one = plane_y(filter_table(LOW_PASS, cols_two, 2 * cols_two, True).T, delta_one)
    returned = lax.all_to_all(
        from_lanes(delta_one, channels), "gy", split_axis=2, concat_axis=3, tiled=True
    )
    rows_back = returned.shape[1]
    margin = from_behind(returned[:, rows_back - 3 :], "gx", 1)
    widened = along_x(
        lifted_table(LOW_PASS, 2 * rows_back, rows_back + 3), jnp.concatenate([margin, returned], 1)
    )
    cols_back = widened.shape[2]
    margin = from_behind(widened[:, :, cols_back - 3 :], "gy", 1)
    delta_zero = along_y(
        lifted_table(LOW_PASS, 2 * cols_back, cols_back + 3), jnp.concatenate([margin, widened], 2)
    )
    return (signal + delta_zero, split_bands)


def local(flow_field, cotangent, mode_weights, point_weights, point_bias):
    channels = flow_field.shape[0]
    modes_x = flow_field.shape[1] * lax.axis_size("gx") // 16
    modes_y = flow_field.shape[2] * lax.axis_size("gy") // 16
    weights_grid = mode_weights.reshape(4, channels, channels, modes_x, modes_y)
    spectral_flow, bands_flow = wave_block(flow_field, weights_grid, False)
    pointwise = jnp.einsum(
        "io,ixys->oxys", point_weights, flow_field, precision=lax.Precision.HIGHEST
    )
    before_gelu = spectral_flow + pointwise + point_bias[:, None, None, None]
    output_field, gelu_slope = gelu_parts(before_gelu)
    grad_inner = cotangent * gelu_slope
    spectral_grad, bands_grad = wave_block(grad_inner, weights_grid, True)
    point_back = jnp.einsum(
        "io,oxys->ixys", point_weights, grad_inner, precision=lax.Precision.HIGHEST
    )
    grad_field = spectral_grad + point_back
    mode_local = jnp.einsum(
        "bizxy,bozxy->bioxy", bands_flow, bands_grad, precision=lax.Precision.HIGHEST
    )
    mode_local = mode_local.reshape(4, channels, channels, modes_x * modes_y)
    mode_total = lax.psum(mode_local, "gy")
    point_local = jnp.einsum(
        "ixys,oxys->io", flow_field, grad_inner, precision=lax.Precision.HIGHEST
    )
    bias_local = jnp.sum(grad_inner, axis=(1, 2, 3))
    point_total, bias_total = lax.psum((point_local, bias_local), ("gx", "gy"))
    plane_total = flow_field.shape[3]
    cell_count = (
        plane_total
        * flow_field.shape[1]
        * flow_field.shape[2]
        * lax.axis_size("gx")
        * lax.axis_size("gy")
    )
    grad_modes = mode_total / math.sqrt(plane_total)
    grad_point = point_total / math.sqrt(cell_count)
    grad_bias = bias_total / math.sqrt(cell_count)
    return (output_field, grad_field, grad_modes, grad_point, grad_bias)


def solution(mesh):
    in_specs = (P(None, "gx", "gy", None), P(None, "gx", "gy", None), P(), P(), P())
    out_specs = (P(None, "gx", "gy", None), P(None, "gx", "gy", None), P(), P(), P())
    return jax.shard_map(local, mesh=mesh, in_specs=in_specs, out_specs=out_specs, check_vma=False)
```

profile of v0, /device:TPU:8, one launch (start us, length us, event | category | flops | bytes accessed | tf_op | source)
XLA Modules:
  0.0 609.2 jit_solution(3356555167298708479)
XLA Ops:
  9.3 6.7 %collective-permute-done = f32[16,6,8,128]{3,1,2,0:T(8,128)S(1)} collective-permute-done((f32[16,6,8,128]{3,1,2,0:T(8,128)S(1)}, f32[16,6,8,128]{3,1,2,0:T(8,128)S(1)}, u32[]{:S(2)}, u32[]{:S(2)}) %collective-permute-start) | collective-permute-done | bytes 393248 | tf_op jit(solution)/shard_map/ppermute | solution.py:24
  17.9 8.1 %collective-permute-start.1 = (f32[16,16,6,128]{3,1,2,0:T(8,128)S(1)}, f32[16,16,6,128]{3,1,2,0:T(8,128)S(1)}, u32[]{:S(2)}, u32[]{:S(2)}) collective-permute-start(f32[16,16,6,128]{3,1,2,0:T(8,128)S(1)} %slice.105), channel_id=1, source_target_pairs={{0,31},{1,0},{2,1},{3,2},{4,3},{5,4},{6,5},{7,6},{8,7},{9,8},{10,9... | collective-permute-start | bytes 2359304 | tf_op jit(solution)/shard_map/ppermute | solution.py:24
  26.0 17.1 %collective-permute-done.1 = f32[16,16,6,128]{3,1,2,0:T(8,128)S(1)} collective-permute-done((f32[16,16,6,128]{3,1,2,0:T(8,128)S(1)}, f32[16,16,6,128]{3,1,2,0:T(8,128)S(1)}, u32[]{:S(2)}, u32[]{:S(2)}) %collective-permute-start.1) | collective-permute-done | bytes 786464 | tf_op jit(solution)/shard_map/ppermute | solution.py:24
  54.1 7.6 %all-to-all-start = ((f32[32,1,4096]{2,1,0:T(1,128)}), f32[32,1,4096]{2,1,0:T(1,128)S(1)}, u32[]{:S(2)}, u32[]{:S(2)}) async-start(f32[32,1,4096]{2,1,0:T(1,128)} %reshape.86), calls=%async_computation | async-start | bytes 1048576 | tf_op jit(solution)/shard_map/all_to_all | solution.py:127
  61.7 6.2 %copy.304 = f32[4,16,16,256]{2,1,3,0:T(8,128)} copy(f32[4,16,16,256]{3,2,1,0:T(8,128)S(1)} %copy-done.4) | data formatting | bytes 2097152 | tf_op jit(solution)/shard_map/reshape | solution.py:188
  68.0 11.4 %all-to-all-done = f32[32,1,4096]{2,1,0:T(1,128)S(1)} async-done(((f32[32,1,4096]{2,1,0:T(1,128)}), f32[32,1,4096]{2,1,0:T(1,128)S(1)}, u32[]{:S(2)}, u32[]{:S(2)}) %all-to-all-start) | async-done | bytes 524320 | tf_op jit(solution)/shard_map/all_to_all | solution.py:127
  105.0 14.3 %all_gather.6 = f32[64,32,32]{0,2,1:T(8,128)S(1)} all-gather(f32[64,4,32]{0,2,1:T(8,128)S(1)} %fusion.123), channel_id=1, replica_groups=mesh['gx'=8,'gy'=32] {'gx'}, dimensions={1}, use_global_device_ids=true | all-gather | bytes 294912 | tf_op jit(solution)/shard_map/all_gather | solution.py:142
  125.7 14.9 %bitcast_subtract_fusion.1 = f32[4,16,4,16,16]{1,2,4,3,0:T(4,128)S(1)} fusion(f32[4,16,16,16,16]{2,1,4,3,0:T(8,128)} %bitcast.264, f32[1,16,4,16,16]{1,2,4,3,0:T(4,128)S(1)} %copy.227, f32[1,16,4,16,16]{1,2,4,3,0:T(4,128)S(1)} %copy.226, f32[1,16,4,16,16]{1,2,4,3,0:T(4,128)S(1)} %copy.225, f32[1,16,4,16,16]{1,2,4,3,0:T(4,128)S(1)} %copy.224), kind=kOutput, calls=%fused_computation.23 | convolution fusion | flops 13041664 | bytes 1572864 | tf_op jit(solution)/shard_map/bizxy,bioxy->bozxy/dot_general | solution.py:151
  175.0 22.0 %all_to_all.72 = f32[32,1,4096]{2,1,0:T(1,128)S(1)} all-to-all(f32[32,1,4096]{2,1,0:T(1,128)S(1)} %reshape.88), channel_id=1, replica_groups=mesh['gx'=8,'gy'=32] {'gy'}, dimensions={0} | all-to-all | bytes 1048576 | tf_op jit(solution)/shard_map/all_to_all | solution.py:168
  220.1 15.0 %collective-permute-done.7 = f32[16,32,3,128]{3,1,2,0:T(8,128)S(1)} collective-permute-done((f32[16,32,3,128]{3,1,2,0:T(8,128)S(1)}, f32[16,32,3,128]{3,1,2,0:T(8,128)S(1)}, u32[]{:S(2)}, u32[]{:S(2)}) %collective-permute-start.7) | collective-permute-done | bytes 786464 | tf_op jit(solution)/shard_map/ppermute | solution.py:24
  235.3 6.6 %fusion.1133 = (f32[16]{0:T(128)}, f32[16,32,8,128]{3,2,1,0:T(8,128)S(1)}, f32[16,32,8,128]{3,2,1,0:T(8,128)}) fusion(f32[16,32,8,128]{3,2,1,0:T(8,128)S(1)} %copy-done.20, f32[16]{0:T(128)S(1)} %copy-done.21, f32[16,32,8,128]{3,0,2,1:T(8,128)S(1)} %fusion.27, f32[16,32,8,128]{3,2,1,0:T(8,128)S(1)} %copy-done.1, s32[7]{0:T(128)S(1)} %iota_multiply_fusion.2, ...), kind=kOutput, calls=%fused_computation.1198 | convolution fusion | flops 56100200 | bytes 12320924 | tf_op jit(solution)/shard_map/kr,axrs->axks/dot_general | solution.py:54
  241.9 5.3 collective-permute-done.8
  249.6 19.6 %collective-permute-done.9 = f32[16,16,6,128]{3,1,2,0:T(8,128)S(1)} collective-permute-done((f32[16,16,6,128]{3,1,2,0:T(8,128)S(1)}, f32[16,16,6,128]{3,1,2,0:T(8,128)S(1)}, u32[]{:S(2)}, u32[]{:S(2)}) %collective-permute-start.9) | collective-permute-done | bytes 786464 | tf_op jit(solution)/shard_map/ppermute | solution.py:24
  279.4 19.5 %all_to_all.73 = f32[32,1,4096]{2,1,0:T(1,128)S(1)} all-to-all(f32[32,1,4096]{2,1,0:T(1,128)S(1)} %reshape.90), channel_id=1, replica_groups=mesh['gx'=8,'gy'=32] {'gy'}, dimensions={0} | all-to-all | bytes 1048576 | tf_op jit(solution)/shard_map/all_to_all | solution.py:127
  319.1 5.1 collective-permute-done.11
  325.1 17.3 %all_gather.7 = f32[64,32,32]{0,2,1:T(8,128)S(1)} all-gather(f32[64,4,32]{0,2,1:T(8,128)S(1)} %fusion.119), channel_id=1, replica_groups=mesh['gx'=8,'gy'=32] {'gx'}, dimensions={1}, use_global_device_ids=true | all-gather | bytes 294912 | tf_op jit(solution)/shard_map/all_gather | solution.py:142
  350.4 18.2 %bitcast_subtract_fusion = f32[4,16,4,16,16]{1,2,4,3,0:T(4,128)S(1)} fusion(f32[4,16,16,16,16]{2,1,4,3,0:T(8,128)} %bitcast.265, f32[1,16,4,16,16]{1,2,4,3,0:T(4,128)} %copy.269, f32[1,16,4,16,16]{1,2,4,3,0:T(4,128)} %copy.268, f32[1,16,4,16,16]{1,2,4,3,0:T(4,128)} %copy.267, f32[1,16,4,16,16]{1,2,4,3,0:T(4,128)S(1)} %copy.266), kind=kOutput, calls=%fused_computation.19 | convolution fusion | flops 13041664 | bytes 1572864 | tf_op jit(solution)/shard_map/bozxy,bioxy->bizxy/dot_general | solution.py:147
  409.7 5.7 all-to-all-start.3
  415.5 17.6 %fusion.86 = f32[4,16,16,16,16]{4,3,2,1,0:T(8,128)} fusion(f32[1,16,4,16,16]{1,2,4,3,0:T(4,128)} %copy.269, f32[1,16,4,16,16]{1,2,4,3,0:T(4,128)} %copy.268, f32[1,16,4,16,16]{1,2,4,3,0:T(4,128)} %copy.267, f32[1,16,4,16,16]{1,2,4,3,0:T(4,128)} %copy-done.10, f32[1,16,4,16,16]{1,2,4,3,0:T(4,128)} %copy-done.9, f32[1,16,4,16,16]{1,2,4,3,0:T(4,128)} %copy-done.7, ...), kind=kOutput, calls=%fused_computation.106 | convolution fusion | flops 12976128 | bytes 1572864 | tf_op jit(solution)/shard_map/bizxy,bozxy->bioxy/dot_general | solution.py:201
  433.0 7.7 %copy.290 = f32[4,16,16,256]{3,2,1,0:T(8,128)} copy(f32[4,16,16,256]{1,2,3,0:T(8,128)} %bitcast.266) | data formatting | bytes 2097152 | tf_op jit(solution)/shard_map/reshape | solution.py:204
  440.8 6.3 %fusion.45 = f32[16,16]{0,1:T(8,128)S(1)} fusion(f32[16,32,8,128]{3,2,1,0:T(8,128)} %param.5, f32[16,32,8,128]{3,2,1,0:T(8,128)S(1)} %get-tuple-element.28), kind=kOutput, calls=%fused_computation.66 | convolution fusion | flops 100663296 | bytes 4195328 | tf_op jit(solution)/shard_map/ixys,oxys->io/dot_general | solution.py:206
  447.1 77.5 %all-reduce = (f32[16,16]{0,1:T(8,128)S(1)}, f32[16]{0:T(128)S(1)}) all-reduce(f32[16,16]{0,1:T(8,128)S(1)} %fusion.45, f32[16]{0:T(128)S(1)} %copy-done.19), channel_id=1, replica_groups=mesh['gx'=8,'gy'=32] {'gx','gy'}, use_global_device_ids=true, to_apply=%region_1.2 | all-reduce | flops 272 | bytes 2176 | tf_op jit(solution)/shard_map/psum | solution.py:210
  551.4 41.4 %all-reduce.3.cloned.1.call-done = f32[4,16,16,256]{3,2,1,0:T(8,128)} async-done(((f32[4,16,16,256]{3,2,1,0:T(8,128)}), f32[4,16,16,256]{3,2,1,0:T(8,128)}) %all-reduce.3.cloned.1.call-update) | async-done | bytes 1048592 | tf_op jit(solution)/shard_map/psum | solution.py:205
  596.9 5.2 bitcast_add_fusion
  (209 shorter events, 217.6 us)
Async XLA Ops:
  7.2 210.0 %copy-start = (f32[16,16]{1,0:T(8,128)S(1)}, f32[16,16]{1,0:T(8,128)}, u32[]{:S(2)}) copy-start(f32[16,16]{1,0:T(8,128)} %param.8) | copy-start | bytes 3076
  9.2 6.7 %collective-permute-start = (f32[16,6,8,128]{3,1,2,0:T(8,128)S(1)}, f32[16,6,8,128]{3,1,2,0:T(8,128)S(1)}, u32[]{:S(2)}, u32[]{:S(2)}) collective-permute-start(f32[16,6,8,128]{3,1,2,0:T(8,128)S(1)} %slice.104), channel_id=1, source_target_pairs={{0,224},{32,0},{64,32},{96,64},{128,96},{160,128},{192,160},{224,1... | collective-permute-start | bytes 1179656 | tf_op jit(solution)/shard_map/ppermute | solution.py:24
  17.9 25.2 %collective-permute-start.1 = (f32[16,16,6,128]{3,1,2,0:T(8,128)S(1)}, f32[16,16,6,128]{3,1,2,0:T(8,128)S(1)}, u32[]{:S(2)}, u32[]{:S(2)}) collective-permute-start(f32[16,16,6,128]{3,1,2,0:T(8,128)S(1)} %slice.105), channel_id=1, source_target_pairs={{0,31},{1,0},{2,1},{3,2},{4,3},{5,4},{6,5},{7,6},{8,7},{9,8},{10,9... | collective-permute-start | bytes 2359304 | tf_op jit(solution)/shard_map/ppermute | solution.py:24
  54.1 25.3 %all-to-all-start = ((f32[32,1,4096]{2,1,0:T(1,128)}), f32[32,1,4096]{2,1,0:T(1,128)S(1)}, u32[]{:S(2)}, u32[]{:S(2)}) async-start(f32[32,1,4096]{2,1,0:T(1,128)} %reshape.86), calls=%async_computation | async-start | bytes 1048576 | tf_op jit(solution)/shard_map/all_to_all | solution.py:127
  93.2 3.9 collective-permute-start.2
  98.2 5.8 collective-permute-start.3
  100.1 224.6 %copy-start.15 = (s32[32]{0:T(128)}, s32[32]{0:T(128)S(1)}, u32[]{:S(2)}) copy-start(s32[32]{0:T(128)S(1)} %iota_multiply_fusion.3) | copy-start | bytes 388
  150.8 5.0 collective-permute-start.4
  150.9 84.3 %copy-start.11 = (s32[7]{0:T(128)}, s32[7]{0:T(128)S(1)}, u32[]{:S(2)}) copy-start(s32[7]{0:T(128)S(1)} %iota_multiply_fusion.2) | copy-start | bytes 88
  156.7 4.1 collective-permute-start.5
  209.3 4.4 collective-permute-start.6
  214.9 20.2 %collective-permute-start.7 = (f32[16,32,3,128]{3,1,2,0:T(8,128)S(1)}, f32[16,32,3,128]{3,1,2,0:T(8,128)S(1)}, u32[]{:S(2)}, u32[]{:S(2)}) collective-permute-start(f32[16,32,3,128]{3,1,2,0:T(8,128)S(1)} %slice.115), channel_id=1, source_target_pairs={{0,1},{1,2},{2,3},{3,4},{4,5},{5,6},{6,7},{7,8},{8,9},{9,10},{10,1... | collective-permute-start | bytes 2359304 | tf_op jit(solution)/shard_map/ppermute | solution.py:24
  220.0 15.2 %copy-start.20 = (f32[16,32,8,128]{3,2,1,0:T(8,128)S(1)}, f32[16,32,8,128]{3,2,1,0:T(8,128)}, u32[]{:S(2)}) copy-start(f32[16,32,8,128]{3,2,1,0:T(8,128)} %param.6) | copy-start | bytes 6291460
  220.0 15.2 %copy-start.21 = (f32[16]{0:T(128)S(1)}, f32[16]{0:T(128)}, u32[]{:S(2)}) copy-start(f32[16]{0:T(128)} %param.9) | copy-start | bytes 196
  241.9 5.3 collective-permute-start.8
  249.5 19.7 %collective-permute-start.9 = (f32[16,16,6,128]{3,1,2,0:T(8,128)S(1)}, f32[16,16,6,128]{3,1,2,0:T(8,128)S(1)}, u32[]{:S(2)}, u32[]{:S(2)}) collective-permute-start(f32[16,16,6,128]{3,1,2,0:T(8,128)S(1)} %slice.117), channel_id=1, source_target_pairs={{0,31},{1,0},{2,1},{3,2},{4,3},{5,4},{6,5},{7,6},{8,7},{9,8},{10,9... | collective-permute-start | bytes 2359304 | tf_op jit(solution)/shard_map/ppermute | solution.py:24
  312.2 3.9 collective-permute-start.10
  317.2 7.0 %collective-permute-start.11 = (f32[64,6,64]{2,1,0:T(8,128)S(1)}, f32[64,6,64]{2,1,0:T(8,128)S(1)}, u32[]{:S(2)}, u32[]{:S(2)}) collective-permute-start(f32[64,6,64]{2,1,0:T(8,128)S(1)} %bitcast.290), channel_id=1, source_target_pairs={{0,224},{32,0},{64,32},{96,64},{128,96},{160,128},{192,160},{224,1... | collective-permute-start | bytes 294920 | tf_op jit(solution)/shard_map/ppermute | solution.py:24
  384.8 5.0 collective-permute-start.12
  390.7 4.1 collective-permute-start.13
  409.7 114.9 %all-to-all-start.3 = ((f32[32,1,4096]{2,1,0:T(1,128)}), f32[32,1,4096]{2,1,0:T(1,128)S(1)}, u32[]{:S(2)}, u32[]{:S(2)}) async-start(f32[32,1,4096]{2,1,0:T(1,128)} %reshape.92), calls=%async_computation.3 | async-start | bytes 1048576 | tf_op jit(solution)/shard_map/all_to_all | solution.py:168
  415.4 177.4 %all-reduce.3.cloned.1.call-start = ((), (), s32[]{:S(2)}) async-start(), calls=%async_computation.4 | async-start | bytes 2097152 | tf_op jit(solution)/shard_map/psum | solution.py:205
  536.9 4.9 collective-permute-start.14
  545.0 50.1 %collective-permute-start.15 = (f32[16,32,3,128]{3,1,2,0:T(8,128)}, f32[16,32,3,128]{3,1,2,0:T(8,128)}, u32[]{:S(2)}, u32[]{:S(2)}) collective-permute-start(f32[16,32,3,128]{3,1,2,0:T(8,128)} %slice.127), channel_id=1, source_target_pairs={{0,1},{1,2},{2,3},{3,4},{4,5},{5,6},{6,7},{7,8},{8,9},{9,10},{10,1... | collective-permute-start | bytes 2359304 | tf_op jit(solution)/shard_map/ppermute | solution.py:24
  (17 other events, 111.1 us)
Sparse Core Ops, SparseCore 0:
  440.9 151.8 all-reduce.2
where the time goes:
time: 616 us; the launch traced here: 609 us
  waiting for transfers between devices  159 us (26%)
  blocking collectives  151 us (25%)
  local copies, waits for them, and re-layouts  122 us (20%)
  matrix products  119 us (19%)
  starting transfers between devices  29.7 us (5%)
  between operations  15.3 us (2%)
  other arithmetic  13.7 us (2%)
    ppermute x16, waiting for transfers between devices, from_behind(): lax.ppermute(value, axis, [(i, (i + by) % devices) for i in range(devices)])  106 us
    psum x1, blocking collectives, local(): point_total, bias_total = lax.psum((point_local, bias_local), ('gx', 'gy'))  77.5 us
    psum x1, waiting for transfers between devices, local(): mode_total = lax.psum(mode_local, 'gy')  41.4 us
    unnamed x56, local copies, waits for them, and re-layouts  40.1 us
    all_gather x2, blocking collectives, wave_block(): gathered = lax.all_gather(level_three, 'gx', axis=1, tiled=True)  31.6 us
    all_to_all x1, blocking collectives, wave_block(): lax.all_to_all(from_lanes(delta_one, channels), 'gy', split_axis=2, conca...  22 us
    dot_general x24, matrix products, plane_y(): jnp.einsum('kr,axr->axk', matrix, signal, precision=lax.Precision.HIGHEST)  20.3 us
    all_to_all x1, blocking collectives, wave_block(): lax.all_to_all(level_one, 'gy', split_axis=3, concat_axis=2, tiled=True)  19.5 us
  transfers between devices with their start and end apart: 19, of which 17 were waited for; matrix products, arithmetic and copies ran while one was open for 11% of the time, Pallas kernels for 0%

commit v1 on v0

--- a/solution.py
+++ b/solution.py
@@ -202,7 +202,11 @@
         "bizxy,bozxy->bioxy", bands_flow, bands_grad, precision=lax.Precision.HIGHEST
     )
     mode_local = mode_local.reshape(4, channels, channels, modes_x * modes_y)
-    mode_total = lax.psum(mode_local, "gy")
+    mode_total = mode_local
+    for hop in (1, 2, 4, 8, 16):
+        mode_total = mode_total + lax.ppermute(
+            mode_total, "gy", [(dev, dev ^ hop) for dev in range(32)]
+        )
     point_local = jnp.einsum(
         "ixys,oxys->io", flow_field, grad_inner, precision=lax.Precision.HIGHEST
     )

time: 616 us -> 678 us (1.10)
  waiting for transfers between devices: 159 us -> 206 us
  between operations: 15.3 us -> 2.15 us
  starting transfers between devices: 29.7 us -> 39.7 us
  other arithmetic: 13.7 us -> 21.1 us
    ppermute x0 -> x5, waiting for transfers between devices: none -> 87.7 us  [local(): lax.ppermute(mode_total, 'gy', [(dev, dev ^ hop) for dev in range(32)])]
    psum x1 -> x0, waiting for transfers between devices: 41.4 us -> none  [local(): mode_total = lax.psum(mode_local, 'gy')]
    ppermute x0 -> x5, starting transfers between devices: none -> 8.77 us  [local(): lax.ppermute(mode_total, 'gy', [(dev, dev ^ hop) for dev in range(32)])]
    add x0 -> x4, other arithmetic: none -> 8.41 us  [local(): mode_total + lax.ppermute(mode_total, 'gy', [(dev, dev ^ hop) for dev in...]
    unnamed x56 -> x66, local copies, waits for them, and re-layouts: 40.1 us -> 40.6 us
  transfers between devices with their start and end apart: 19 -> 23, of which waited for: 17 -> 20; matrix products, arithmetic and copies ran while one was open for 11% -> 13% of each run, Pallas kernels for 0% -> 0%
where the time goes in v1:
time: 678 us; the launch traced here: 670 us
  waiting for transfers between devices  206 us (30%)
  blocking collectives  154 us (23%)
  local copies, waits for them, and re-layouts  127 us (19%)
  matrix products  120 us (18%)
  starting transfers between devices  39.7 us (6%)
  other arithmetic  21.1 us (3%)
    ppermute x16, waiting for transfers between devices, from_behind(): lax.ppermute(value, axis, [(i, (i + by) % devices) for i in range(devices)])  101 us
    ppermute x5, waiting for transfers between devices, local(): lax.ppermute(mode_total, 'gy', [(dev, dev ^ hop) for dev in range(32)])  87.7 us
    psum x1, blocking collectives, local(): point_total, bias_total = lax.psum((point_local, bias_local), ('gx', 'gy'))  80.7 us
    unnamed x66, local copies, waits for them, and re-layouts  40.6 us
    all_gather x2, blocking collectives, wave_block(): gathered = lax.all_gather(level_three, 'gx', axis=1, tiled=True)  31.6 us
    dot_general x24, matrix products, plane_y(): jnp.einsum('kr,axr->axk', matrix, signal, precision=lax.Precision.HIGHEST)  22.5 us
    all_to_all x1, blocking collectives, wave_block(): lax.all_to_all(from_lanes(delta_one, channels), 'gy', split_axis=2, conca...  22.1 us
    dot_general x1, matrix products, wave_block(): jnp.einsum('bozxy,bioxy->bizxy', split_bands, weights_grid, precision=lax...  20.2 us
  transfers between devices with their start and end apart: 23, of which 20 were waited for; matrix products, arithmetic and copies ran while one was open for 13% of the time, Pallas kernels for 0%

profile of v1, /device:TPU:8, one launch (start us, length us, event | category | flops | bytes accessed | tf_op | source)
XLA Modules:
  0.0 670.0 jit_solution(13528114457484593911)
XLA Ops:
  2.7 6.7 collective-permute-done
  11.3 8.1 %collective-permute-start.1 = (f32[16,16,6,128]{3,1,2,0:T(8,128)S(1)}, f32[16,16,6,128]{3,1,2,0:T(8,128)S(1)}, u32[]{:S(2)}, u32[]{:S(2)}) collective-permute-start(f32[16,16,6,128]{3,1,2,0:T(8,128)S(1)} %slice.105), channel_id=1, source_target_pairs={{0,31},{1,0},{2,1},{3,2},{4,3},{5,4},{6,5},{7,6},{8,7},{9,8},{10,9... | collective-permute-start | bytes 2359304 | tf_op jit(solution)/shard_map/ppermute | solution.py:24
  19.5 17.1 %collective-permute-done.1 = f32[16,16,6,128]{3,1,2,0:T(8,128)S(1)} collective-permute-done((f32[16,16,6,128]{3,1,2,0:T(8,128)S(1)}, f32[16,16,6,128]{3,1,2,0:T(8,128)S(1)}, u32[]{:S(2)}, u32[]{:S(2)}) %collective-permute-start.1) | collective-permute-done | bytes 786464 | tf_op jit(solution)/shard_map/ppermute | solution.py:24
  47.6 7.7 %all-to-all-start = ((f32[32,1,4096]{2,1,0:T(1,128)}), f32[32,1,4096]{2,1,0:T(1,128)S(1)}, u32[]{:S(2)}, u32[]{:S(2)}) async-start(f32[32,1,4096]{2,1,0:T(1,128)} %reshape.86), calls=%async_computation | async-start | bytes 1048576 | tf_op jit(solution)/shard_map/all_to_all | solution.py:127
  55.3 6.2 copy.308
  61.5 11.4 %all-to-all-done = f32[32,1,4096]{2,1,0:T(1,128)S(1)} async-done(((f32[32,1,4096]{2,1,0:T(1,128)}), f32[32,1,4096]{2,1,0:T(1,128)S(1)}, u32[]{:S(2)}, u32[]{:S(2)}) %all-to-all-start) | async-done | bytes 524320 | tf_op jit(solution)/shard_map/all_to_all | solution.py:127
  98.5 14.5 %all_gather.6 = f32[64,32,32]{0,2,1:T(8,128)S(1)} all-gather(f32[64,4,32]{0,2,1:T(8,128)S(1)} %fusion.123), channel_id=1, replica_groups=mesh['gx'=8,'gy'=32] {'gx'}, dimensions={1}, use_global_device_ids=true | all-gather | bytes 294912 | tf_op jit(solution)/shard_map/all_gather | solution.py:142
  119.4 14.6 %bitcast_subtract_fusion.1 = f32[4,16,4,16,16]{1,2,4,3,0:T(4,128)S(1)} fusion(f32[4,16,16,16,16]{2,1,4,3,0:T(8,128)} %bitcast.264, f32[1,16,4,16,16]{1,2,4,3,0:T(4,128)S(1)} %copy.230, f32[1,16,4,16,16]{1,2,4,3,0:T(4,128)S(1)} %copy.229, f32[1,16,4,16,16]{1,2,4,3,0:T(4,128)S(1)} %copy.228, f32[1,16,4,16,16]{1,2,4,3,0:T(4,128)S(1)} %copy.227), kind=kOutput, calls=%fused_computation.23 | convolution fusion | flops 13041664 | bytes 1572864 | tf_op jit(solution)/shard_map/bizxy,bioxy->bozxy/dot_general | solution.py:151
  168.6 22.1 %all_to_all.72 = f32[32,1,4096]{2,1,0:T(1,128)S(1)} all-to-all(f32[32,1,4096]{2,1,0:T(1,128)S(1)} %reshape.88), channel_id=1, replica_groups=mesh['gx'=8,'gy'=32] {'gy'}, dimensions={0} | all-to-all | bytes 1048576 | tf_op jit(solution)/shard_map/all_to_all | solution.py:168
  213.7 15.0 %collective-permute-done.7 = f32[16,32,3,128]{3,1,2,0:T(8,128)S(1)} collective-permute-done((f32[16,32,3,128]{3,1,2,0:T(8,128)S(1)}, f32[16,32,3,128]{3,1,2,0:T(8,128)S(1)}, u32[]{:S(2)}, u32[]{:S(2)}) %collective-permute-start.7) | collective-permute-done | bytes 786464 | tf_op jit(solution)/shard_map/ppermute | solution.py:24
  229.0 6.8 %fusion.1133 = (f32[16]{0:T(128)}, f32[16,32,8,128]{3,2,1,0:T(8,128)S(1)}, f32[16,32,8,128]{3,2,1,0:T(8,128)}) fusion(f32[16,32,8,128]{3,2,1,0:T(8,128)S(1)} %copy-done.25, f32[16]{0:T(128)S(1)} %copy-done.26, f32[16,32,8,128]{3,0,2,1:T(8,128)S(1)} %fusion.27, f32[16,32,8,128]{3,2,1,0:T(8,128)S(1)} %copy-done.1, s32[7]{0:T(128)S(1)} %iota_multiply_fusion.2, ...), kind=kOutput, calls=%fused_computation.1198 | convolution fusion | flops 56100200 | bytes 12320924 | tf_op jit(solution)/shard_map/kr,axrs->axks/dot_general | solution.py:54
  235.8 5.3 collective-permute-done.8
  243.5 19.6 %collective-permute-done.9 = f32[16,16,6,128]{3,1,2,0:T(8,128)S(1)} collective-permute-done((f32[16,16,6,128]{3,1,2,0:T(8,128)S(1)}, f32[16,16,6,128]{3,1,2,0:T(8,128)S(1)}, u32[]{:S(2)}, u32[]{:S(2)}) %collective-permute-start.9) | collective-permute-done | bytes 786464 | tf_op jit(solution)/shard_map/ppermute | solution.py:24
  273.3 19.4 %all_to_all.73 = f32[32,1,4096]{2,1,0:T(1,128)S(1)} all-to-all(f32[32,1,4096]{2,1,0:T(1,128)S(1)} %reshape.90), channel_id=1, replica_groups=mesh['gx'=8,'gy'=32] {'gy'}, dimensions={0} | all-to-all | bytes 1048576 | tf_op jit(solution)/shard_map/all_to_all | solution.py:127
  319.1 17.2 %all_gather.7 = f32[64,32,32]{0,2,1:T(8,128)S(1)} all-gather(f32[64,4,32]{0,2,1:T(8,128)S(1)} %fusion.119), channel_id=1, replica_groups=mesh['gx'=8,'gy'=32] {'gx'}, dimensions={1}, use_global_device_ids=true | all-gather | bytes 294912 | tf_op jit(solution)/shard_map/all_gather | solution.py:142
  345.0 17.7 %fusion.86 = f32[4,16,16,16,16]{4,3,2,1,0:T(8,128)} fusion(f32[1,16,4,16,16]{1,2,4,3,0:T(4,128)} %copy.272, f32[1,16,4,16,16]{1,2,4,3,0:T(4,128)} %copy.271, f32[1,16,4,16,16]{1,2,4,3,0:T(4,128)} %copy.270, f32[1,16,4,16,16]{1,2,4,3,0:T(4,128)} %copy.269, f32[1,16,4,16,16]{1,2,4,3,0:T(4,128)} %copy-done.11, f32[1,16,4,16,16]{1,2,4,3,0:T(4,128)} %copy-done.9, ...), kind=kOutput, calls=%fused_computation.106 | convolution fusion | flops 12976128 | bytes 1572864 | tf_op jit(solution)/shard_map/bizxy,bozxy->bioxy/dot_general | solution.py:201
  362.7 20.2 %bitcast_subtract_fusion = f32[4,16,4,16,16]{1,2,4,3,0:T(4,128)} fusion(f32[4,16,16,16,16]{2,1,4,3,0:T(8,128)} %bitcast.265, f32[1,16,4,16,16]{1,2,4,3,0:T(4,128)S(1)} %copy-done.15, f32[1,16,4,16,16]{1,2,4,3,0:T(4,128)S(1)} %copy-done.13, f32[1,16,4,16,16]{1,2,4,3,0:T(4,128)S(1)} %copy-done.14, f32[1,16,4,16,16]{1,2,4,3,0:T(4,128)S(1)} %copy-done.12), kind=kOutput, calls=%fused_computation.19 | convolution fusion | flops 13041664 | bytes 1572864 | tf_op jit(solution)/shard_map/bozxy,bioxy->bizxy/dot_general | solution.py:147
  383.0 6.5 copy.294
  431.5 36.4 %collective-permute-done.17 = f32[4,16,16,256]{3,2,1,0:T(8,128)} collective-permute-done((f32[4,16,16,256]{3,2,1,0:T(8,128)}, f32[4,16,16,256]{3,2,1,0:T(8,128)}, u32[]{:S(2)}, u32[]{:S(2)}) %collective-permute-start.17) | collective-permute-done | bytes 1048608 | tf_op jit(solution)/shard_map/ppermute | solution.py:207
  480.3 7.2 %all-to-all-start.3 = ((f32[32,1,4096]{2,1,0:T(1,128)}), f32[32,1,4096]{2,1,0:T(1,128)}, u32[]{:S(2)}, u32[]{:S(2)}) async-start(f32[32,1,4096]{2,1,0:T(1,128)} %reshape.92), calls=%async_computation.3 | async-start | bytes 1048576 | tf_op jit(solution)/shard_map/all_to_all | solution.py:168
  487.5 35.5 %collective-permute-done.18 = f32[4,16,16,256]{3,2,1,0:T(8,128)} collective-permute-done((f32[4,16,16,256]{3,2,1,0:T(8,128)S(1)}, f32[4,16,16,256]{3,2,1,0:T(8,128)}, u32[]{:S(2)}, u32[]{:S(2)}) %collective-permute-start.18) | collective-permute-done | bytes 1048608 | tf_op jit(solution)/shard_map/ppermute | solution.py:207
  526.1 5.9 all-to-all-done.3
  558.8 80.7 %all-reduce = (f32[16,16]{0,1:T(8,128)S(1)}, f32[16]{0:T(128)S(1)}) all-reduce(f32[16,16]{0,1:T(8,128)S(1)} %fusion.45, f32[16]{0:T(128)S(1)} %copy-done.24), channel_id=1, replica_groups=mesh['gx'=8,'gy'=32] {'gx','gy'}, use_global_device_ids=true, to_apply=%region_0.1 | all-reduce | flops 272 | bytes 2176 | tf_op jit(solution)/shard_map/psum | solution.py:214
  654.0 14.4 %collective-permute-done.20 = f32[4,16,16,256]{3,2,1,0:T(8,128)S(1)} collective-permute-done((f32[4,16,16,256]{3,2,1,0:T(8,128)S(1)}, f32[4,16,16,256]{3,2,1,0:T(8,128)S(1)}, u32[]{:S(2)}, u32[]{:S(2)}) %collective-permute-start.20) | collective-permute-done | bytes 1048608 | tf_op jit(solution)/shard_map/ppermute | solution.py:207
  (230 shorter events, 251.7 us)
Async XLA Ops:
  2.7 6.7 %collective-permute-start = (f32[16,6,8,128]{3,1,2,0:T(8,128)S(1)}, f32[16,6,8,128]{3,1,2,0:T(8,128)S(1)}, u32[]{:S(2)}, u32[]{:S(2)}) collective-permute-start(f32[16,6,8,128]{3,1,2,0:T(8,128)S(1)} %slice.104), channel_id=1, source_target_pairs={{0,224},{32,0},{64,32},{96,64},{128,96},{160,128},{192,160},{224,1... | collective-permute-start | bytes 1179656 | tf_op jit(solution)/shard_map/ppermute | solution.py:24
  11.3 25.2 %collective-permute-start.1 = (f32[16,16,6,128]{3,1,2,0:T(8,128)S(1)}, f32[16,16,6,128]{3,1,2,0:T(8,128)S(1)}, u32[]{:S(2)}, u32[]{:S(2)}) collective-permute-start(f32[16,16,6,128]{3,1,2,0:T(8,128)S(1)} %slice.105), channel_id=1, source_target_pairs={{0,31},{1,0},{2,1},{3,2},{4,3},{5,4},{6,5},{7,6},{8,7},{9,8},{10,9... | collective-permute-start | bytes 2359304 | tf_op jit(solution)/shard_map/ppermute | solution.py:24
  47.6 25.3 %all-to-all-start = ((f32[32,1,4096]{2,1,0:T(1,128)}), f32[32,1,4096]{2,1,0:T(1,128)S(1)}, u32[]{:S(2)}, u32[]{:S(2)}) async-start(f32[32,1,4096]{2,1,0:T(1,128)} %reshape.86), calls=%async_computation | async-start | bytes 1048576 | tf_op jit(solution)/shard_map/all_to_all | solution.py:127
  86.7 3.9 collective-permute-start.2
  91.7 5.8 collective-permute-start.3
  93.6 225.0 %copy-start.20 = (s32[32]{0:T(128)}, s32[32]{0:T(128)S(1)}, u32[]{:S(2)}) copy-start(s32[32]{0:T(128)S(1)} %iota_multiply_fusion.3) | copy-start | bytes 388
  144.3 5.0 collective-permute-start.4
  150.2 4.1 collective-permute-start.5
  203.0 4.4 collective-permute-start.6
  208.6 20.2 %collective-permute-start.7 = (f32[16,32,3,128]{3,1,2,0:T(8,128)S(1)}, f32[16,32,3,128]{3,1,2,0:T(8,128)S(1)}, u32[]{:S(2)}, u32[]{:S(2)}) collective-permute-start(f32[16,32,3,128]{3,1,2,0:T(8,128)S(1)} %slice.115), channel_id=1, source_target_pairs={{0,1},{1,2},{2,3},{3,4},{4,5},{5,6},{6,7},{7,8},{8,9},{9,10},{10,1... | collective-permute-start | bytes 2359304 | tf_op jit(solution)/shard_map/ppermute | solution.py:24
  235.8 5.3 collective-permute-start.8
  243.4 19.7 %collective-permute-start.9 = (f32[16,16,6,128]{3,1,2,0:T(8,128)S(1)}, f32[16,16,6,128]{3,1,2,0:T(8,128)S(1)}, u32[]{:S(2)}, u32[]{:S(2)}) collective-permute-start(f32[16,16,6,128]{3,1,2,0:T(8,128)S(1)} %slice.117), channel_id=1, source_target_pairs={{0,31},{1,0},{2,1},{3,2},{4,3},{5,4},{6,5},{7,6},{8,7},{9,8},{10,9... | collective-permute-start | bytes 2359304 | tf_op jit(solution)/shard_map/ppermute | solution.py:24
  306.0 3.9 collective-permute-start.10
  311.0 7.1 %collective-permute-start.11 = (f32[64,6,64]{2,1,0:T(8,128)S(1)}, f32[64,6,64]{2,1,0:T(8,128)S(1)}, u32[]{:S(2)}, u32[]{:S(2)}) collective-permute-start(f32[64,6,64]{2,1,0:T(8,128)S(1)} %bitcast.290), channel_id=1, source_target_pairs={{0,224},{32,0},{64,32},{96,64},{128,96},{160,128},{192,160},{224,1... | collective-permute-start | bytes 294920 | tf_op jit(solution)/shard_map/ppermute | solution.py:24
  389.5 26.6 %collective-permute-start.16 = (f32[4,16,16,256]{3,2,1,0:T(8,128)S(1)}, f32[4,16,16,256]{3,2,1,0:T(8,128)}, u32[]{:S(2)}, u32[]{:S(2)}) collective-permute-start(f32[4,16,16,256]{3,2,1,0:T(8,128)S(1)} %copy.294), channel_id=1, source_target_pairs={{0,1},{1,0},{2,3},{3,2},{4,5},{5,4},{6,7},{7,6},{8,9},{9,8},{10,11... | collective-permute-start | bytes 3145736 | tf_op jit(solution)/shard_map/ppermute | solution.py:207
  414.7 5.4 collective-permute-start.12
  418.5 49.4 %collective-permute-start.17 = (f32[4,16,16,256]{3,2,1,0:T(8,128)}, f32[4,16,16,256]{3,2,1,0:T(8,128)}, u32[]{:S(2)}, u32[]{:S(2)}) collective-permute-start(f32[4,16,16,256]{3,2,1,0:T(8,128)} %add.1263), channel_id=1, source_target_pairs={{0,2},{1,3},{2,0},{3,1},{4,6},{5,7},{6,4},{7,5},{8,10},{9,11},{10,... | collective-permute-start | bytes 3145736 | tf_op jit(solution)/shard_map/ppermute | solution.py:207
  421.0 4.4 collective-permute-start.13
  469.7 53.3 %collective-permute-start.18 = (f32[4,16,16,256]{3,2,1,0:T(8,128)S(1)}, f32[4,16,16,256]{3,2,1,0:T(8,128)}, u32[]{:S(2)}, u32[]{:S(2)}) collective-permute-start(f32[4,16,16,256]{3,2,1,0:T(8,128)S(1)} %add.1264), channel_id=1, source_target_pairs={{0,4},{1,5},{2,6},{3,7},{4,0},{5,1},{6,2},{7,3},{8,12},{9,13},{10,... | collective-permute-start | bytes 3145736 | tf_op jit(solution)/shard_map/ppermute | solution.py:207
  480.3 51.7 %all-to-all-start.3 = ((f32[32,1,4096]{2,1,0:T(1,128)}), f32[32,1,4096]{2,1,0:T(1,128)}, u32[]{:S(2)}, u32[]{:S(2)}) async-start(f32[32,1,4096]{2,1,0:T(1,128)} %reshape.92), calls=%async_computation.3 | async-start | bytes 1048576 | tf_op jit(solution)/shard_map/all_to_all | solution.py:168
  525.5 114.7 %collective-permute-start.19 = (f32[4,16,16,256]{3,2,1,0:T(8,128)}, f32[4,16,16,256]{3,2,1,0:T(8,128)}, u32[]{:S(2)}, u32[]{:S(2)}) collective-permute-start(f32[4,16,16,256]{3,2,1,0:T(8,128)} %add.1265), channel_id=1, source_target_pairs={{0,8},{1,9},{2,10},{3,11},{4,12},{5,13},{6,14},{7,15},{8,0},{9,1},... | collective-permute-start | bytes 3145736 | tf_op jit(solution)/shard_map/ppermute | solution.py:207
  545.5 4.4 collective-permute-start.14
  553.0 94.4 %collective-permute-start.15 = (f32[16,32,3,128]{3,1,2,0:T(8,128)}, f32[16,32,3,128]{3,1,2,0:T(8,128)}, u32[]{:S(2)}, u32[]{:S(2)}) collective-permute-start(f32[16,32,3,128]{3,1,2,0:T(8,128)} %slice.127), channel_id=1, source_target_pairs={{0,1},{1,2},{2,3},{3,4},{4,5},{5,6},{6,7},{7,8},{8,9},{9,10},{10,1... | collective-permute-start | bytes 2359304 | tf_op jit(solution)/shard_map/ppermute | solution.py:24
  641.9 26.5 %collective-permute-start.20 = (f32[4,16,16,256]{3,2,1,0:T(8,128)S(1)}, f32[4,16,16,256]{3,2,1,0:T(8,128)S(1)}, u32[]{:S(2)}, u32[]{:S(2)}) collective-permute-start(f32[4,16,16,256]{3,2,1,0:T(8,128)S(1)} %add.1266), channel_id=1, source_target_pairs={{0,16},{1,17},{2,18},{3,19},{4,20},{5,21},{6,22},{7,23},{8,24},{9,... | collective-permute-start | bytes 3145736 | tf_op jit(solution)/shard_map/ppermute | solution.py:207
  (26 other events, 500.1 us)
